TPU v7x, 32 devices: a whole 2x2x4 slice. The times are simulated.
32 devices in a mesh: frames: 8 (over z, x), heads: 4 (over y, core).
Axes of the slice: x: 2, y: 2, z: 4, core: 2. Of those that a mesh axis runs over, the one named last changes fastest.
Arguments:
- queries: bfloat16 [1024, 4096], P('frames', 'heads'), may hold values from -9 to 9
- keys: bfloat16 [1024, 512], P(('frames', 'heads')), may hold values from -4.5 to 4.5
- values: bfloat16 [1024, 512], P(('frames', 'heads')), may hold values from -6 to 6
- block_mask: int32 [8, 8], replicated, may hold values from 0 to 1, as said below
- lengths: int32 [8], replicated, may hold values from 64 to 128, as said below
Outputs:
- attended: bfloat16 [1024, 4096], P('frames', 'heads')
Inputs may be any that keep to these rules, and one draw needn't show every extreme that they name: block_mask[i, i] = 1 and block_mask[i, j] = 0 for j > i. `lengths`: some frame group is full in every draw.
All inputs are finite; a program needn't handle non-finite values.
Results may differ from a plain program's by a relative error of at most 0.0055.
Values may be sent and summed in bfloat16 or wider, within the bound.
A program may use at most 64 MiB of HBM per device.

v0:
```python
import math
import jax
import jax.numpy as jnp
from jax import lax
from jax.sharding import PartitionSpec as P

HEAD_DIM = 128
masked_score = -1e30


def attend(query_sets, keys_mine, values_mine, block_mask, lengths, group_tokens):
    kv_local = keys_mine.shape[1] // HEAD_DIM
    q_local = query_sets[0][0].shape[1] // HEAD_DIM
    per_kv = q_local // kv_local
    scale = HEAD_DIM ** (-0.5)
    group_count = block_mask.shape[0]
    group_ids = jnp.arange(group_count, dtype=jnp.int32)
    prepared = []
    initial = []
    for rows, owner in query_sets:
        count = rows.shape[0]
        prepared.append(
            (
                rows.reshape(count, kv_local, per_kv, HEAD_DIM),
                lax.dynamic_slice_in_dim(block_mask, owner, 1, 0)[0],
            )
        )
        initial.append(
            (
                jnp.full((kv_local, per_kv, count), masked_score, jnp.float32),
                jnp.zeros((kv_local, per_kv, count), jnp.float32),
                jnp.zeros((count, kv_local, per_kv, HEAD_DIM), jnp.float32),
            )
        )
    key_piece = lax.all_gather(keys_mine, "frames", axis=0, tiled=True)
    value_piece = lax.all_gather(values_mine, "frames", axis=0, tiled=True)
    fold_rows = key_piece.shape[0]
    width = math.gcd(fold_rows, 512)
    blocks = fold_rows // width
    key_blocks = key_piece.reshape(blocks, width, kv_local, HEAD_DIM)
    value_blocks = value_piece.reshape(blocks, width, kv_local, HEAD_DIM)

    def one_block(state, inputs):
        key_block, value_block, number = inputs
        positions = number * width + jnp.arange(width, dtype=jnp.int32)
        key_group = positions // group_tokens
        within = positions % group_tokens
        onehot = (key_group[:, None] == group_ids[None, :]).astype(jnp.int32)
        live_len = jnp.sum(onehot * lengths[None, :], axis=1)
        updated = []
        for (query_rows, mask_row), (running_max, running_total, running_acc) in zip(
            prepared, state
        ):
            allowed = jnp.sum(onehot * mask_row[None, :], axis=1)
            valid = (allowed > 0) & (within < live_len)

            def update(current):
                old_max, old_total, old_acc = current
                scores = (
                    jnp.einsum(
                        "tkgd,skd->kgts", query_rows, key_block, preferred_element_type=jnp.float32
                    )
                    * scale
                )
                scores = jnp.where(valid[None, None, None, :], scores, masked_score)
                new_max = jnp.maximum(old_max, jnp.max(scores, axis=-1))
                probs = jnp.exp(scores - new_max[..., None])
                factor = jnp.exp(old_max - new_max)
                new_total = old_total * factor + jnp.sum(probs, axis=-1)
                added = jnp.einsum(
                    "kgts,skd->tkgd",
                    probs.astype(jnp.bfloat16),
                    value_block,
                    preferred_element_type=jnp.float32,
                )
                new_acc = old_acc * jnp.transpose(factor, (2, 0, 1))[..., None] + added
                return (new_max, new_total, new_acc)

            updated.append(
                lax.cond(
                    jnp.any(valid),
                    update,
                    lambda current: current,
                    (running_max, running_total, running_acc),
                )
            )
        return (tuple(updated), None)

    numbers = jnp.arange(blocks, dtype=jnp.int32)
    final, unused = lax.scan(one_block, tuple(initial), (key_blocks, value_blocks, numbers))
    results = []
    for (rows, owner), (running_max, running_total, running_acc) in zip(query_sets, final):
        output = running_acc / jnp.transpose(running_total, (2, 0, 1))[..., None]
        results.append(output.astype(jnp.bfloat16).reshape(rows.shape[0], q_local * HEAD_DIM))
    return results


def local(queries, keys, values, block_mask, lengths):
    keys_mine, values_mine = (
        lax.all_to_all(keys, "heads", split_axis=1, concat_axis=0, tiled=True),
        lax.all_to_all(values, "heads", split_axis=1, concat_axis=0, tiled=True),
    )
    group_tokens = queries.shape[0]
    frame_index = lax.axis_index("frames")
    outputs = attend(
        [(queries, frame_index)], keys_mine, values_mine, block_mask, lengths, group_tokens
    )
    return outputs[0]


def solution(mesh):
    return jax.shard_map(
        local,
        mesh=mesh,
        in_specs=(
            P("frames", "heads"),
            P(("frames", "heads"), None),
            P(("frames", "heads"), None),
            P(),
            P(),
        ),
        out_specs=P("frames", "heads"),
        check_vma=False,
    )
```

profile of v0, /device:TPU:30, one launch (start us, length us, event | category | flops | bytes accessed | tf_op | source)
XLA Modules:
  0.0 84.3 jit_solution(984634713009666700)
XLA Ops:
  0.0 0.0 copy-start
  0.0 0.8 copy-done
  0.8 0.6 copy_bitcast_fusion
  1.4 3.7 %all-to-all-start.1 = ((bf16[32,4,128]{2,0,1:T(8,128)(2,1)}), bf16[32,4,128]{2,0,1:T(8,128)(2,1)S(1)}, u32[]{:S(2)}, u32[]{:S(2)}) async-start(bf16[32,4,128]{2,0,1:T(8,128)(2,1)} %copy_bitcast_fusion), calls=%async_computation.1 | async-start | bytes 65536 | tf_op jit(solution)/shard_map/all_to_all | solution.py:101
  5.1 1.4 %copy_bitcast_fusion.1 = bf16[32,4,128]{2,0,1:T(8,128)(2,1)} fusion(bf16[32,512]{1,0:T(8,128)(2,1)} %param.10), kind=kLoop, calls=%fused_computation.47 | loop fusion | bytes 65536 | tf_op jit(solution)/shard_map/all_to_all | solution.py:100
  6.5 0.7 constant_dynamic-slice_fusion
  7.2 1.1 %copy.37 = bf16[128,1024]{0,1:T(8,128)(2,1)S(1)} copy(bf16[128,1024]{1,0:T(8,128)(2,1)} %param.9) | data formatting | bytes 524288 | tf_op args[0]
  8.3 0.2 copy.39
  8.5 0.0 all-to-all-done.1
  8.5 3.8 %all-to-all-start = ((bf16[32,4,128]{2,0,1:T(8,128)(2,1)}), bf16[32,4,128]{2,0,1:T(8,128)(2,1)S(1)}, u32[]{:S(2)}, u32[]{:S(2)}) async-start(bf16[32,4,128]{2,0,1:T(8,128)(2,1)} %copy_bitcast_fusion.1), calls=%async_computation | async-start | bytes 65536 | tf_op jit(solution)/shard_map/all_to_all | solution.py:100
  12.3 30.8 %all_gather.7 = bf16[1024,128]{1,0:T(8,128)(2,1)S(1)} all-gather(bf16[128,128]{1,0:T(8,128)(2,1)S(1)} %bitcast.97), channel_id=1, replica_groups=mesh['frames'=8,'heads'=4] {'frames'}, dimensions={0}, use_global_device_ids=true | all-gather | bytes 294912 | tf_op jit(solution)/shard_map/all_gather | solution.py:36
  43.1 0.1 copy.40
  43.3 0.0 all-to-all-done
  43.3 30.7 %all_gather.6 = bf16[1024,128]{1,0:T(8,128)(2,1)S(1)} all-gather(bf16[128,128]{1,0:T(8,128)(2,1)S(1)} %bitcast.98), channel_id=1, replica_groups=mesh['frames'=8,'heads'=4] {'frames'}, dimensions={0}, use_global_device_ids=true | all-gather | bytes 294912 | tf_op jit(solution)/shard_map/all_gather | solution.py:35
  74.1 0.0 copy-done.1
  74.1 9.3 %while.17 = (s32[]{:T(128)}, f32[1,8,128]{2,1,0:T(8,128)S(1)}, f32[1,8,128]{2,1,0:T(8,128)S(1)}, f32[128,1,8,128]{0,3,2,1:T(8,128)S(1)}, s32[2]{0:T(128)S(1)}, /...) while((s32[]{:T(128)}, f32[1,8,128]{2,1,0:T(8,128)S(1)}, ...), condition=%wide.region_8.9_spmd.clone, body=%wide.region_0.8_spmd.clone.sunk | while | flops 274503680 | bytes 7944539 | solution.py:90
  74.1 0.6 dynamic_slice.43
  75.3 0.1 fusion.38
  75.4 0.7 fusion.39
  76.9 1.9 %conditional.3 = ((f32[1,8,128]{2,1,0:T(8,128)S(1)}, f32[1,8,128]{2,1,0:T(8,128)S(1)}, f32[128,1,8,128]{0,3,2,1:T(8,128)S(1)})) conditional(s32[]{:T(128)} %convert_element_type.23, (f32[1,8,128]{2,1,0:T(8,128)S(1)}, f32[1,8,128]{2,1,0:T(8,128)S(1)}, f32[128,1,8,128]{0,3,2,1:T(8,128)S(1)}) %tuple.59, (pred[512]{0:T(512)(128)(4,1)S(1)}, ...), branch_computations={%region_4.4_spmd, %region_5.7_spmd} | conditional | flops 274467840 | bytes 7931432 | solution.py:80
  76.9 0.5 bitcast_reduce_fusion
  77.4 0.8 fusion.5
  78.2 0.5 fusion.4
  78.7 0.6 dynamic_slice.43
  80.0 0.1 fusion.38
  80.1 0.7 fusion.39
  81.5 1.9 %conditional.3 = ((f32[1,8,128]{2,1,0:T(8,128)S(1)}, f32[1,8,128]{2,1,0:T(8,128)S(1)}, f32[128,1,8,128]{0,3,2,1:T(8,128)S(1)})) conditional(s32[]{:T(128)} %convert_element_type.23, (f32[1,8,128]{2,1,0:T(8,128)S(1)}, f32[1,8,128]{2,1,0:T(8,128)S(1)}, f32[128,1,8,128]{0,3,2,1:T(8,128)S(1)}) %tuple.59, (pred[512]{0:T(512)(128)(4,1)S(1)}, ...), branch_computations={%region_4.4_spmd, %region_5.7_spmd} | conditional | flops 274467840 | bytes 7931432 | solution.py:80
  81.5 0.5 bitcast_reduce_fusion
  82.0 0.8 fusion.5
  82.9 0.5 fusion.4
  83.4 0.1 divide_convert_fusion
  83.5 0.9 %copy.43 = bf16[128,1024]{1,0:T(8,128)(2,1)} copy(bf16[128,1024]{0,1:T(8,128)(2,1)S(1)} %bitcast.93) | data formatting | bytes 524288 | tf_op jit(solution)/shard_map/reshape | solution.py:94
  (13 shorter events, 0.1 us)
Async XLA Ops:
  0.0 0.8 copy-start
  0.8 73.3 %copy-start.1 = (s32[8]{0:T(128)S(1)}, s32[8]{0:T(128)}, u32[]{:S(2)}) copy-start(s32[8]{0:T(128)} %param.13) | copy-start | bytes 100
  1.4 7.1 %all-to-all-start.1 = ((bf16[32,4,128]{2,0,1:T(8,128)(2,1)}), bf16[32,4,128]{2,0,1:T(8,128)(2,1)S(1)}, u32[]{:S(2)}, u32[]{:S(2)}) async-start(bf16[32,4,128]{2,0,1:T(8,128)(2,1)} %copy_bitcast_fusion), calls=%async_computation.1 | async-start | bytes 65536 | tf_op jit(solution)/shard_map/all_to_all | solution.py:101
  8.5 34.8 %all-to-all-start = ((bf16[32,4,128]{2,0,1:T(8,128)(2,1)}), bf16[32,4,128]{2,0,1:T(8,128)(2,1)S(1)}, u32[]{:S(2)}, u32[]{:S(2)}) async-start(bf16[32,4,128]{2,0,1:T(8,128)(2,1)} %copy_bitcast_fusion.1), calls=%async_computation | async-start | bytes 65536 | tf_op jit(solution)/shard_map/all_to_all | solution.py:100
where the time goes:
time: 84.8 us; the launch traced here: 84.3 us
  blocking collectives  61.6 us (73%)
  starting transfers between devices  7.53 us (9%)
  local copies, waits for them, and re-layouts  6.95 us (8%)
  loops' own time  2.87 us (3%)
  other arithmetic  2.72 us (3%)
  matrix products  2.59 us (3%)
    all_gather x1, blocking collectives, attend(): value_piece = lax.all_gather(values_mine, 'frames', axis=0, tiled=True)  30.8 us
    all_gather x1, blocking collectives, attend(): key_piece = lax.all_gather(keys_mine, 'frames', axis=0, tiled=True)  30.7 us
    all_to_all x1, starting transfers between devices, local(): lax.all_to_all(keys, 'heads', split_axis=1, concat_axis=0, tiled=True)  3.79 us
    all_to_all x1, starting transfers between devices, local(): lax.all_to_all(values, 'heads', split_axis=1, concat_axis=0, tiled=True)  3.74 us
    another operation x1, loops' own time, attend(): lax.scan(one_block, tuple(initial), (key_blocks, value_blocks, numbers))  2.76 us
    unnamed x7, local copies, waits for them, and re-layouts  2.2 us
  transfers between devices with their start and end apart: 2, of which 0 were waited for; matrix products, arithmetic and copies ran while one was open for 4% of the time, Pallas kernels for 0%

commit v1 on v0

--- a/solution.py
+++ b/solution.py
@@ -32,7 +32,9 @@
                 jnp.zeros((count, kv_local, per_kv, HEAD_DIM), jnp.float32),
             )
         )
-    key_piece = lax.all_gather(keys_mine, "frames", axis=0, tiled=True)
+    key_piece = jnp.concatenate(
+        lax.all_to_all(jnp.stack([keys_mine] * lax.axis_size("frames")), "frames", 0, 0), axis=0
+    )
     value_piece = lax.all_gather(values_mine, "frames", axis=0, tiled=True)
     fold_rows = key_piece.shape[0]
     width = math.gcd(fold_rows, 512)

time: 84.8 us -> 65 us (0.77)
  the two profiles are of different devices: /device:TPU:30 before, /device:TPU:26 now
where the time goes in v1:
time: 65 us; the launch traced here: 64.4 us
  blocking collectives  37 us (57%)
  starting transfers between devices  9.26 us (14%)
  local copies, waits for them, and re-layouts  7.1 us (11%)
  waiting for transfers between devices  3.15 us (5%)
  loops' own time  2.61 us (4%)
  matrix products  2.59 us (4%)
  other arithmetic  2.55 us (4%)
    all_gather x1, blocking collectives, attend(): value_piece = lax.all_gather(values_mine, 'frames', axis=0, tiled=True)  30.7 us
    all_to_all x1, blocking collectives, local(): lax.all_to_all(keys, 'heads', split_axis=1, concat_axis=0, tiled=True)  6.29 us
    all_to_all x1, starting transfers between devices, attend(): lax.all_to_all(jnp.stack([keys_mine] * lax.axis_size('frames')), 'frames'...  6 us
    all_to_all x1, starting transfers between devices, local(): lax.all_to_all(values, 'heads', split_axis=1, concat_axis=0, tiled=True)  3.26 us
    all_to_all x1, waiting for transfers between devices, local(): lax.all_to_all(values, 'heads', split_axis=1, concat_axis=0, tiled=True)  3.14 us
    another operation x1, loops' own time, attend(): lax.scan(one_block, tuple(initial), (key_blocks, value_blocks, numbers))  2.5 us
    unnamed x7, local copies, waits for them, and re-layouts  2.2 us
    dot_general x2, matrix products, update(): jnp.einsum('kgts,skd->tkgd', probs.astype(jnp.bfloat16), value_block, pre...  1.68 us
  transfers between devices with their start and end apart: 2, of which 1 were waited for; matrix products, arithmetic and copies ran while one was open for 5% of the time, Pallas kernels for 0%

profile of v1, /device:TPU:26, one launch (start us, length us, event | category | flops | bytes accessed | tf_op | source)
XLA Modules:
  0.0 64.4 jit_solution(6874277777161926)
XLA Ops:
  0.0 0.0 copy-start
  0.0 0.8 %copy-done = bf16[32,512]{1,0:T(8,128)(2,1)S(1)} copy-done((bf16[32,512]{1,0:T(8,128)(2,1)S(1)}, bf16[32,512]{1,0:T(8,128)(2,1)}, u32[]{:S(2)}) %copy-start) | copy-done | bytes 32792
  0.8 0.6 copy_bitcast_fusion
  1.4 3.3 %all-to-all-start.2 = ((bf16[32,4,128]{2,0,1:T(8,128)(2,1)}), bf16[32,4,128]{2,0,1:T(8,128)(2,1)S(1)}, u32[]{:S(2)}, u32[]{:S(2)}) async-start(bf16[32,4,128]{2,0,1:T(8,128)(2,1)} %copy_bitcast_fusion), calls=%async_computation.2 | async-start | bytes 65536 | tf_op jit(solution)/shard_map/all_to_all | solution.py:103
  4.7 0.8 %copy_bitcast_fusion.1 = bf16[32,4,128]{2,0,1:T(8,128)(2,1)S(1)} fusion(bf16[32,512]{1,0:T(8,128)(2,1)} %param.10), kind=kLoop, calls=%fused_computation.47 | loop fusion | bytes 65536 | tf_op jit(solution)/shard_map/all_to_all | solution.py:102
  5.4 3.1 %all-to-all-done.2 = bf16[32,4,128]{2,0,1:T(8,128)(2,1)S(1)} async-done(((bf16[32,4,128]{2,0,1:T(8,128)(2,1)}), bf16[32,4,128]{2,0,1:T(8,128)(2,1)S(1)}, u32[]{:S(2)}, u32[]{:S(2)}) %all-to-all-start.2) | async-done | bytes 32800 | tf_op jit(solution)/shard_map/all_to_all | solution.py:103
  8.6 6.3 %all_to_all.40 = bf16[32,4,128]{2,0,1:T(8,128)(2,1)S(1)} all-to-all(bf16[32,4,128]{2,0,1:T(8,128)(2,1)S(1)} %copy_bitcast_fusion.1), channel_id=1, replica_groups=mesh['frames'=8,'heads'=4] {'heads'}, dimensions={1} | all-to-all | bytes 65536 | tf_op jit(solution)/shard_map/all_to_all | solution.py:102
  14.9 0.7 %stack.5 = bf16[8,128,128]{2,1,0:T(8,128)(2,1)} broadcast(bf16[128,128]{1,0:T(8,128)(2,1)S(1)} %bitcast.98), dimensions={1,2} | broadcast | bytes 294912 | tf_op jit(solution)/shard_map/stack | solution.py:36
  15.6 6.0 %all-to-all-start.1 = ((bf16[8,128,128]{2,1,0:T(8,128)(2,1)}), bf16[8,128,128]{2,1,0:T(8,128)(2,1)S(1)}, u32[]{:S(2)}, u32[]{:S(2)}) async-start(bf16[8,128,128]{2,1,0:T(8,128)(2,1)} %stack.5), calls=%async_computation.1 | async-start | bytes 524288 | tf_op jit(solution)/shard_map/all_to_all | solution.py:36
  21.6 1.1 %copy.29 = bf16[128,1024]{0,1:T(8,128)(2,1)S(1)} copy(bf16[128,1024]{1,0:T(8,128)(2,1)} %param.9) | data formatting | bytes 524288 | tf_op args[0]
  22.7 0.2 copy.31
  22.9 0.7 %constant_dynamic-slice_fusion = s32[1,8]{1,0:T(1,128)S(1)} fusion(s32[8,8]{1,0:T(8,128)} %param.12, s32[]{:T(128)S(6)} %select_n.36), kind=kLoop, calls=%fused_computation.48 | loop fusion | bytes 68 | tf_op jit(solution)/shard_map/dynamic_slice | solution.py:25
  23.6 30.7 %all_gather.3 = bf16[1024,128]{1,0:T(8,128)(2,1)S(1)} all-gather(bf16[128,128]{1,0:T(8,128)(2,1)S(1)} %bitcast.97), channel_id=1, replica_groups=mesh['frames'=8,'heads'=4] {'frames'}, dimensions={0}, use_global_device_ids=true | all-gather | bytes 294912 | tf_op jit(solution)/shard_map/all_gather | solution.py:38
  54.3 0.1 copy.32
  54.5 0.0 all-to-all-done.1
  54.6 8.9 %while.17 = (s32[]{:T(128)}, f32[1,8,128]{2,1,0:T(8,128)S(1)}, f32[1,8,128]{2,1,0:T(8,128)S(1)}, f32[128,1,8,128]{0,3,2,1:T(8,128)S(1)}, s32[2]{0:T(128)S(1)}, /...) while((s32[]{:T(128)}, f32[1,8,128]{2,1,0:T(8,128)S(1)}, ...), condition=%wide.region_8.9_spmd.clone, body=%wide.region_0.8_spmd.clone.sunk | while | flops 274503680 | bytes 7944539 | solution.py:92
  54.6 0.6 dynamic_slice.43
  55.9 0.1 fusion.38
  55.9 0.6 fusion.39
  57.2 1.9 %conditional.3 = ((f32[1,8,128]{2,1,0:T(8,128)S(1)}, f32[1,8,128]{2,1,0:T(8,128)S(1)}, f32[128,1,8,128]{0,3,2,1:T(8,128)S(1)})) conditional(s32[]{:T(128)} %convert_element_type.23, (f32[1,8,128]{2,1,0:T(8,128)S(1)}, f32[1,8,128]{2,1,0:T(8,128)S(1)}, f32[128,1,8,128]{0,3,2,1:T(8,128)S(1)}) %tuple.58, (pred[512]{0:T(512)(128)(4,1)S(1)}, ...), branch_computations={%region_4.4_spmd, %region_5.7_spmd} | conditional | flops 274467840 | bytes 7931432 | solution.py:82
  57.2 0.5 bitcast_reduce_fusion
  57.7 0.8 %fusion.5 = f32[128,1,8,128]{0,3,2,1:T(8,128)S(1)} fusion(f32[512,128,8]{1,0,2:T(8,128)S(1)} %get-tuple-element.322, f32[8,128]{1,0:T(8,128)S(1)} %bitcast.91, pred[512]{0:T(512)(128)(4,1)S(1)} %get-tuple-element.204, f32[128,1,8,128]{0,3,2,1:T(8,128)S(1)} %get-tuple-element.209, f32[128,8]{0,1:T(8,128)S(1)} %get-tuple-element.317, ...), kind=kOutput, calls=%fused_computation.8 | convolution fusion | flops 136577024 | bytes 3285508 | tf_op jit(solution)/shard_map/while/body/eval_jaxpr/cond/branch_1_fun/kgts,skd->tkgd/dot_general | solution.py:72
  58.5 0.5 fusion.4
  59.0 0.6 dynamic_slice.43
  60.3 0.1 fusion.38
  60.4 0.6 fusion.39
  61.6 1.9 %conditional.3 = ((f32[1,8,128]{2,1,0:T(8,128)S(1)}, f32[1,8,128]{2,1,0:T(8,128)S(1)}, f32[128,1,8,128]{0,3,2,1:T(8,128)S(1)})) conditional(s32[]{:T(128)} %convert_element_type.23, (f32[1,8,128]{2,1,0:T(8,128)S(1)}, f32[1,8,128]{2,1,0:T(8,128)S(1)}, f32[128,1,8,128]{0,3,2,1:T(8,128)S(1)}) %tuple.58, (pred[512]{0:T(512)(128)(4,1)S(1)}, ...), branch_computations={%region_4.4_spmd, %region_5.7_spmd} | conditional | flops 274467840 | bytes 7931432 | solution.py:82
  61.6 0.5 bitcast_reduce_fusion
  62.1 0.8 %fusion.5 = f32[128,1,8,128]{0,3,2,1:T(8,128)S(1)} fusion(f32[512,128,8]{1,0,2:T(8,128)S(1)} %get-tuple-element.322, f32[8,128]{1,0:T(8,128)S(1)} %bitcast.91, pred[512]{0:T(512)(128)(4,1)S(1)} %get-tuple-element.204, f32[128,1,8,128]{0,3,2,1:T(8,128)S(1)} %get-tuple-element.209, f32[128,8]{0,1:T(8,128)S(1)} %get-tuple-element.317, ...), kind=kOutput, calls=%fused_computation.8 | convolution fusion | flops 136577024 | bytes 3285508 | tf_op jit(solution)/shard_map/while/body/eval_jaxpr/cond/branch_1_fun/kgts,skd->tkgd/dot_general | solution.py:72
  62.9 0.5 fusion.4
  63.5 0.1 divide_convert_fusion
  63.5 0.9 %copy.35 = bf16[128,1024]{1,0:T(8,128)(2,1)} copy(bf16[128,1024]{0,1:T(8,128)(2,1)S(1)} %bitcast.93) | data formatting | bytes 524288 | tf_op jit(solution)/shard_map/reshape | solution.py:96
  (14 shorter events, 0.1 us)
Async XLA Ops:
  0.0 0.8 %copy-start = (bf16[32,512]{1,0:T(8,128)(2,1)S(1)}, bf16[32,512]{1,0:T(8,128)(2,1)}, u32[]{:S(2)}) copy-start(bf16[32,512]{1,0:T(8,128)(2,1)} %param.11) | copy-start | bytes 98308
  0.8 53.8 %copy-start.1 = (s32[8]{0:T(128)S(1)}, s32[8]{0:T(128)}, u32[]{:S(2)}) copy-start(s32[8]{0:T(128)} %param.13) | copy-start | bytes 100
  1.4 7.2 %all-to-all-start.2 = ((bf16[32,4,128]{2,0,1:T(8,128)(2,1)}), bf16[32,4,128]{2,0,1:T(8,128)(2,1)S(1)}, u32[]{:S(2)}, u32[]{:S(2)}) async-start(bf16[32,4,128]{2,0,1:T(8,128)(2,1)} %copy_bitcast_fusion), calls=%async_computation.2 | async-start | bytes 65536 | tf_op jit(solution)/shard_map/all_to_all | solution.py:103
  15.6 38.9 %all-to-all-start.1 = ((bf16[8,128,128]{2,1,0:T(8,128)(2,1)}), bf16[8,128,128]{2,1,0:T(8,128)(2,1)S(1)}, u32[]{:S(2)}, u32[]{:S(2)}) async-start(bf16[8,128,128]{2,1,0:T(8,128)(2,1)} %stack.5), calls=%async_computation.1 | async-start | bytes 524288 | tf_op jit(solution)/shard_map/all_to_all | solution.py:36
